TPU v7x, 512 devices: a whole 4x8x8 slice. The times are simulated.
512 devices in a mesh: zone: 32 (over x, z_hi, core), period: 16 (over y, z_lo).
Axes of the slice: x: 4, y: 8, z: 8 (z_hi: 4, z_lo: 2; z = z_hi * 2 + z_lo), core: 2. Of those that a mesh axis runs over, the one named last changes fastest.
Arguments:
- x_start: float32 [256, 16, 1600], P('zone', 'period'), may hold values from -6 to 6
- duals: float32 [256, 16, 512], P('zone', 'period'), may hold values from -3 to 3
- cost: float32 [256, 16, 1600], P('zone', 'period'), may hold values from -6 to 6
- hinv: bfloat16 [256, 1600, 1600], P('zone', 'period')
- zone_sizes: int32 [256], P('zone'), may hold values from 640 to 1600, as said below
- partners: int32 [4, 256], P(None, 'zone'), may hold values from 0 to 7, as said below
Outputs:
- primal: float32 [256, 16, 1600], P('zone', 'period')
- dual_out: float32 [256, 16, 512], P('zone', 'period')
Inputs may be any that keep to these rules, and one draw needn't show every extreme that they name: `zone_sizes`: each zone has at least its tie and ramp entries live; some zone uses all 1600. In round r the zones of zone index i are paired one to one with the zones of index i XOR 2**(r mod b), b the log2 of the number of zone indices; partners[r, z] is the partner's position among the 8 zones of its index, and the pairing is mutual.
All inputs are finite; a program needn't handle non-finite values.
Results may differ from a plain program's by a relative error of at most 0.0032.
Values may be sent and summed in bfloat16 or wider, within the bound.
No kernel may reach another device: no remote copies, remote signals or barrier semaphores. Data moves between devices by JAX's collectives and lax.ppermute only.
A program may use at most 64 MiB of HBM per device.

v0:
```python
import jax
import jax.numpy as jnp
from jax import lax
from jax.sharding import PartitionSpec as P

W = 128
G = 128
ROUNDS = 4
ITERS = 2
rho_ties = 1.0
prox_weight = 0.5
ramp_weight = 0.5


def from_partner(block, axis, apart):
    count = lax.axis_size(axis)
    route = []
    for low in range(count):
        high = low | 1 << apart
        if high != low and high < count:
            route += [(low, high), (high, low)]
    return lax.ppermute(block, axis, route)


def padded_2(cells, sides, width):
    for axis, dim in sides:
        count = lax.axis_size(axis)
        ends = count - 1
        head = lax.slice_in_dim(cells, 0, width, axis=dim)
        tail = lax.slice_in_dim(cells, cells.shape[dim] - width, cells.shape[dim], axis=dim)
        cells = jnp.concatenate(
            [
                lax.ppermute(tail, axis, [(i, (i + 1) % count) for i in range(ends)]),
                cells,
                lax.ppermute(head, axis, [((i + 1) % count, i) for i in range(ends)]),
            ],
            axis=dim,
        )
    return cells


def shards(x_start, duals, cost, hinv, zone_sizes, partners):
    zones_here = x_start.shape[0]
    width_total = x_start.shape[2]
    nbits = lax.axis_size("zone").bit_length() - 1
    live_mask = (lax.iota(jnp.int32, width_total)[None, :] < zone_sizes[:, None]).astype(
        jnp.float32
    )[:, None, :]
    tie_end = ROUNDS * W
    current = x_start
    dual_state = duals
    for iteration in range(ITERS):
        tie_terms = []
        new_duals = []
        for round_index in range(ROUNDS):
            own_block = current[:, :, round_index * W : (round_index + 1) * W]
            received = from_partner(own_block, "zone", round_index % nbits)
            partner_block = jnp.take(received, partners[round_index], axis=0)
            old_dual = dual_state[:, :, round_index * W : (round_index + 1) * W]
            updated = old_dual + rho_ties * 0.5 * (own_block - partner_block)
            new_duals.append(updated)
            tie_terms.append(rho_ties * 0.5 * (own_block + partner_block) - updated)
        dual_state = jnp.concatenate(new_duals, axis=2)
        ramp_block = current[:, :, tie_end : tie_end + G]
        padded = padded_2(ramp_block, (("period", 1),), 1)
        ramp_term = ramp_weight * (padded[:, 0:1] + padded[:, 2:3])
        filler = jnp.zeros((zones_here, 1, width_total - tie_end - G), jnp.float32)
        addition = jnp.concatenate(tie_terms + [ramp_term, filler], axis=2)
        right_side = ((prox_weight * current - cost + addition) * live_mask).astype(jnp.bfloat16)
        row_products = jnp.einsum(
            "zpv,zrv->zpr",
            lax.all_gather(right_side, "period", axis=1, tiled=True),
            hinv,
            preferred_element_type=jnp.float32,
        )
        product = lax.all_to_all(row_products, "period", split_axis=1, concat_axis=2, tiled=True)
        current = product * live_mask
    return (current, dual_state)


def solution(mesh):
    placed = (
        P("zone", "period", None),
        P("zone", "period", None),
        P("zone", "period", None),
        P("zone", "period", None),
        P("zone"),
        P(None, "zone"),
    )
    return jax.shard_map(
        shards,
        mesh=mesh,
        in_specs=placed,
        out_specs=(P("zone", "period", None), P("zone", "period", None)),
        check_vma=False,
    )
```

profile of v0, /device:TPU:6, one launch (start us, length us, event | category | flops | bytes accessed | tf_op | source)
XLA Modules:
  0.0 158.9 jit_solution(9922141693585990498)
XLA Ops:
  0.6 0.0 copy-start
  0.6 0.0 copy-start.2
  0.7 1.0 copy.10
  1.6 6.1 %collective-permute-start.1 = (f32[8,1,128]{2,0,1:T(8,128)S(1)}, f32[8,1,128]{2,0,1:T(8,128)S(1)}, u32[]{:S(2)}, u32[]{:S(2)}) collective-permute-start(f32[8,1,128]{2,0,1:T(8,128)S(1)} %get-tuple-element.30), channel_id=1, source_target_pairs={{0,32},{32,0},{16,48},{48,16},{64,96},{96,64},{80,112},{112,80},{1... | collective-permute-start | bytes 12296 | tf_op jit(solution)/shard_map/ppermute | solution.py:22
  7.7 1.9 %collective-permute-start = (f32[8,1,128]{2,0,1:T(8,128)S(1)}, f32[8,1,128]{2,0,1:T(8,128)S(1)}, u32[]{:S(2)}, u32[]{:S(2)}) collective-permute-start(f32[8,1,128]{2,0,1:T(8,128)S(1)} %get-tuple-element.31), channel_id=1, source_target_pairs={{0,16},{16,0},{32,48},{48,32},{64,80},{80,64},{96,112},{112,96},{1... | collective-permute-start | bytes 12296 | tf_op jit(solution)/shard_map/ppermute | solution.py:22
  9.6 0.8 compare_and_fusion
  10.5 0.7 fusion.11
  11.2 0.0 collective-permute-done.1
  11.3 0.6 gather_fusion.1
  11.8 0.0 collective-permute-done
  11.8 0.0 copy-start.1
  11.8 0.6 gather_fusion
  12.4 0.1 constant_dynamic-update-slice_fusion.5
  12.5 0.1 fusion.9
  12.5 2.7 %collective-permute-start.3 = (f32[8,1,128]{2,0,1:T(8,128)S(1)}, f32[8,1,128]{2,0,1:T(8,128)S(1)}, u32[]{:S(2)}, u32[]{:S(2)}) collective-permute-start(f32[8,1,128]{2,0,1:T(8,128)S(1)} %get-tuple-element.28), channel_id=1, source_target_pairs={{0,128},{128,0},{16,144},{144,16},{32,160},{160,32},{48,176},{176,... | collective-permute-start | bytes 12296 | tf_op jit(solution)/shard_map/ppermute | solution.py:22
  15.3 9.1 %collective-permute-start.2 = (f32[8,1,128]{2,0,1:T(8,128)S(1)}, f32[8,1,128]{2,0,1:T(8,128)S(1)}, u32[]{:S(2)}, u32[]{:S(2)}) collective-permute-start(f32[8,1,128]{2,0,1:T(8,128)S(1)} %get-tuple-element.29), channel_id=1, source_target_pairs={{0,64},{64,0},{16,80},{80,16},{32,96},{96,32},{48,112},{112,48},{1... | collective-permute-start | bytes 12296 | tf_op jit(solution)/shard_map/ppermute | solution.py:22
  24.4 1.3 collective-permute-start.5
  25.7 4.5 %collective-permute-start.4 = (f32[8,1,128]{2,0,1:T(8,128)S(1)}, f32[8,1,128]{2,0,1:T(8,128)S(1)}, u32[]{:S(2)}, u32[]{:S(2)}) collective-permute-start(f32[8,1,128]{2,0,1:T(8,128)S(1)} %get-tuple-element.26), channel_id=1, source_target_pairs={{0,1},{1,2},{2,3},{3,4},{4,5},{5,6},{6,7},{7,8},{8,9},{9,10},{10,1... | collective-permute-start | bytes 12296 | tf_op jit(solution)/shard_map/ppermute | solution.py:33
  30.3 0.0 collective-permute-done.3
  30.3 0.6 gather_fusion.3
  30.8 0.0 collective-permute-done.2
  30.9 0.6 gather_fusion.2
  31.4 0.1 constant_dynamic-update-slice_fusion.3
  31.5 0.1 constant_dynamic-update-slice_fusion.2
  31.6 0.0 collective-permute-done.5
  31.6 0.0 collective-permute-done.4
  31.6 0.9 select_convert_fusion.1
  32.5 37.4 %all_gather.6 = bf16[8,16,1600]{2,0,1:T(8,128)(2,1)S(1)} all-gather(bf16[8,1,1600]{2,0,1:T(8,128)(2,1)S(1)} %select_convert_fusion.1), channel_id=1, replica_groups=mesh['zone'=32,'period'=16] {'period'}, dimensions={1}, use_global_device_ids=true | all-gather | bytes 435200 | tf_op jit(solution)/shard_map/all_gather | solution.py:72
  69.9 0.0 copy-done
  69.9 0.9 fusion.2
  70.8 15.9 %all_to_all.24 = f32[8,16,100]{2,0,1:T(8,128)S(1)} all-to-all(f32[8,16,100]{2,0,1:T(8,128)S(1)} %copy.23), channel_id=1, replica_groups=mesh['zone'=32,'period'=16] {'period'}, dimensions={1} | all-to-all | bytes 102400 | tf_op jit(solution)/shard_map/all_to_all | solution.py:76
  86.7 0.1 all_to_all.9
  86.8 0.1 fusion.7
  86.9 2.9 %collective-permute-start.7 = (f32[8,1,128]{2,0,1:T(8,128)S(1)}, f32[8,1,128]{2,0,1:T(8,128)S(1)}, u32[]{:S(2)}, u32[]{:S(2)}) collective-permute-start(f32[8,1,128]{2,0,1:T(8,128)S(1)} %get-tuple-element.24), channel_id=1, source_target_pairs={{0,32},{32,0},{16,48},{48,16},{64,96},{96,64},{80,112},{112,80},{1... | collective-permute-start | bytes 12296 | tf_op jit(solution)/shard_map/ppermute | solution.py:22
  89.8 1.9 %collective-permute-start.6 = (f32[8,1,128]{2,0,1:T(8,128)S(1)}, f32[8,1,128]{2,0,1:T(8,128)S(1)}, u32[]{:S(2)}, u32[]{:S(2)}) collective-permute-start(f32[8,1,128]{2,0,1:T(8,128)S(1)} %get-tuple-element.25), channel_id=1, source_target_pairs={{0,16},{16,0},{32,48},{48,32},{64,80},{80,64},{96,112},{112,96},{1... | collective-permute-start | bytes 12296 | tf_op jit(solution)/shard_map/ppermute | solution.py:22
  91.8 1.6 collective-permute-done.7
  93.3 0.6 gather_fusion.5
  93.9 0.0 collective-permute-done.6
  93.9 0.6 gather_fusion.4
  94.4 0.1 constant_dynamic-update-slice_fusion.11
  94.5 0.1 constant_dynamic-update-slice_fusion.10
  94.6 3.1 %collective-permute-start.9 = (f32[8,1,128]{2,0,1:T(8,128)S(1)}, f32[8,1,128]{2,0,1:T(8,128)S(1)}, u32[]{:S(2)}, u32[]{:S(2)}) collective-permute-start(f32[8,1,128]{2,0,1:T(8,128)S(1)} %get-tuple-element.22), channel_id=1, source_target_pairs={{0,128},{128,0},{16,144},{144,16},{32,160},{160,32},{48,176},{176,... | collective-permute-start | bytes 12296 | tf_op jit(solution)/shard_map/ppermute | solution.py:22
  97.7 1.9 %collective-permute-start.8 = (f32[8,1,128]{2,0,1:T(8,128)S(1)}, f32[8,1,128]{2,0,1:T(8,128)S(1)}, u32[]{:S(2)}, u32[]{:S(2)}) collective-permute-start(f32[8,1,128]{2,0,1:T(8,128)S(1)} %get-tuple-element.23), channel_id=1, source_target_pairs={{0,64},{64,0},{16,80},{80,16},{32,96},{96,32},{48,112},{112,48},{1... | collective-permute-start | bytes 12296 | tf_op jit(solution)/shard_map/ppermute | solution.py:22
  99.6 1.3 collective-permute-start.11
  100.9 4.5 %collective-permute-start.10 = (f32[8,1,128]{2,0,1:T(8,128)S(1)}, f32[8,1,128]{2,0,1:T(8,128)S(1)}, u32[]{:S(2)}, u32[]{:S(2)}) collective-permute-start(f32[8,1,128]{2,0,1:T(8,128)S(1)} %get-tuple-element.21), channel_id=1, source_target_pairs={{0,1},{1,2},{2,3},{3,4},{4,5},{5,6},{6,7},{7,8},{8,9},{9,10},{10,1... | collective-permute-start | bytes 12296 | tf_op jit(solution)/shard_map/ppermute | solution.py:33
  105.5 0.0 collective-permute-done.9
  105.5 0.6 gather_fusion.7
  106.1 1.0 collective-permute-done.8
  107.1 0.6 gather_fusion.6
  107.7 0.1 constant_dynamic-update-slice_fusion.9
  107.7 0.1 constant_dynamic-update-slice_fusion.8
  107.8 0.0 collective-permute-done.11
  107.8 0.0 collective-permute-done.10
  107.9 0.0 copy-done.1
  107.9 0.1 select_convert_fusion
  108.0 33.2 %all_gather.7 = bf16[8,16,1600]{2,0,1:T(8,128)(2,1)S(1)} all-gather(bf16[8,1,1600]{2,0,1:T(8,128)(2,1)S(1)} %select_convert_fusion), channel_id=1, replica_groups=mesh['zone'=32,'period'=16] {'period'}, dimensions={1}, use_global_device_ids=true | all-gather | bytes 435200 | tf_op jit(solution)/shard_map/all_gather | solution.py:72
  141.2 0.9 fusion
  142.0 0.7 copy.28
  142.7 6.3 %all-to-all-start.1 = ((f32[8,16,100]{2,0,1:T(8,128)}), f32[8,16,100]{2,0,1:T(8,128)S(1)}, u32[]{:S(2)}, u32[]{:S(2)}) async-start(f32[8,16,100]{2,0,1:T(8,128)} %copy.28), calls=%async_computation.1 | async-start | bytes 131072 | tf_op jit(solution)/shard_map/all_to_all | solution.py:76
  149.0 0.6 copy.31
  149.6 8.4 %all-to-all-done.1 = f32[8,16,100]{2,0,1:T(8,128)S(1)} async-done(((f32[8,16,100]{2,0,1:T(8,128)}), f32[8,16,100]{2,0,1:T(8,128)S(1)}, u32[]{:S(2)}, u32[]{:S(2)}) %all-to-all-start.1) | async-done | bytes 51232 | tf_op jit(solution)/shard_map/all_to_all | solution.py:76
  158.1 0.1 all_to_all.21
  158.1 0.1 fusion.6
  158.2 0.7 copy.30
  (14 shorter events, 0.1 us)
Async XLA Ops:
  0.6 69.3 %copy-start = (bf16[8,100,1600]{2,0,1:T(8,128)(2,1)S(1)}, bf16[8,100,1600]{2,0,1:T(8,128)(2,1)}, u32[]{:S(2)}) copy-start(bf16[8,100,1600]{2,0,1:T(8,128)(2,1)} %param.11) | copy-start | bytes 7680004
  0.6 86.2 %copy-start.2 = (s32[8]{0:T(128)S(1)}, s32[8]{0:T(128)}, u32[]{:S(2)}) copy-start(s32[8]{0:T(128)} %param.12) | copy-start | bytes 100
  1.6 9.6 %collective-permute-start.1 = (f32[8,1,128]{2,0,1:T(8,128)S(1)}, f32[8,1,128]{2,0,1:T(8,128)S(1)}, u32[]{:S(2)}, u32[]{:S(2)}) collective-permute-start(f32[8,1,128]{2,0,1:T(8,128)S(1)} %get-tuple-element.30), channel_id=1, source_target_pairs={{0,32},{32,0},{16,48},{48,16},{64,96},{96,64},{80,112},{112,80},{1... | collective-permute-start | bytes 12296 | tf_op jit(solution)/shard_map/ppermute | solution.py:22
  7.7 4.1 %collective-permute-start = (f32[8,1,128]{2,0,1:T(8,128)S(1)}, f32[8,1,128]{2,0,1:T(8,128)S(1)}, u32[]{:S(2)}, u32[]{:S(2)}) collective-permute-start(f32[8,1,128]{2,0,1:T(8,128)S(1)} %get-tuple-element.31), channel_id=1, source_target_pairs={{0,16},{16,0},{32,48},{48,32},{64,80},{80,64},{96,112},{112,96},{1... | collective-permute-start | bytes 12296 | tf_op jit(solution)/shard_map/ppermute | solution.py:22
  11.8 96.0 %copy-start.1 = (f32[8,1,1600]{2,1,0:T(1,128)S(1)}, f32[8,1,1600]{2,1,0:T(1,128)}, u32[]{:S(2)}) copy-start(f32[8,1,1600]{2,1,0:T(1,128)} %param.10) | copy-start | bytes 153604
  12.5 17.7 %collective-permute-start.3 = (f32[8,1,128]{2,0,1:T(8,128)S(1)}, f32[8,1,128]{2,0,1:T(8,128)S(1)}, u32[]{:S(2)}, u32[]{:S(2)}) collective-permute-start(f32[8,1,128]{2,0,1:T(8,128)S(1)} %get-tuple-element.28), channel_id=1, source_target_pairs={{0,128},{128,0},{16,144},{144,16},{32,160},{160,32},{48,176},{176,... | collective-permute-start | bytes 12296 | tf_op jit(solution)/shard_map/ppermute | solution.py:22
  15.3 15.6 %collective-permute-start.2 = (f32[8,1,128]{2,0,1:T(8,128)S(1)}, f32[8,1,128]{2,0,1:T(8,128)S(1)}, u32[]{:S(2)}, u32[]{:S(2)}) collective-permute-start(f32[8,1,128]{2,0,1:T(8,128)S(1)} %get-tuple-element.29), channel_id=1, source_target_pairs={{0,64},{64,0},{16,80},{80,16},{32,96},{96,32},{48,112},{112,48},{1... | collective-permute-start | bytes 12296 | tf_op jit(solution)/shard_map/ppermute | solution.py:22
  24.4 7.1 %collective-permute-start.5 = (f32[8,1,128]{2,0,1:T(8,128)S(1)}, f32[8,1,128]{2,0,1:T(8,128)S(1)}, u32[]{:S(2)}, u32[]{:S(2)}) collective-permute-start(f32[8,1,128]{2,0,1:T(8,128)S(1)} %get-tuple-element.26), channel_id=1, source_target_pairs={{1,0},{2,1},{3,2},{4,3},{5,4},{6,5},{7,6},{8,7},{9,8},{10,9},{11,1... | collective-permute-start | bytes 12296 | tf_op jit(solution)/shard_map/ppermute | solution.py:35
  25.7 5.9 %collective-permute-start.4 = (f32[8,1,128]{2,0,1:T(8,128)S(1)}, f32[8,1,128]{2,0,1:T(8,128)S(1)}, u32[]{:S(2)}, u32[]{:S(2)}) collective-permute-start(f32[8,1,128]{2,0,1:T(8,128)S(1)} %get-tuple-element.26), channel_id=1, source_target_pairs={{0,1},{1,2},{2,3},{3,4},{4,5},{5,6},{6,7},{7,8},{8,9},{9,10},{10,1... | collective-permute-start | bytes 12296 | tf_op jit(solution)/shard_map/ppermute | solution.py:33
  86.9 6.4 %collective-permute-start.7 = (f32[8,1,128]{2,0,1:T(8,128)S(1)}, f32[8,1,128]{2,0,1:T(8,128)S(1)}, u32[]{:S(2)}, u32[]{:S(2)}) collective-permute-start(f32[8,1,128]{2,0,1:T(8,128)S(1)} %get-tuple-element.24), channel_id=1, source_target_pairs={{0,32},{32,0},{16,48},{48,16},{64,96},{96,64},{80,112},{112,80},{1... | collective-permute-start | bytes 12296 | tf_op jit(solution)/shard_map/ppermute | solution.py:22
  89.8 4.1 %collective-permute-start.6 = (f32[8,1,128]{2,0,1:T(8,128)S(1)}, f32[8,1,128]{2,0,1:T(8,128)S(1)}, u32[]{:S(2)}, u32[]{:S(2)}) collective-permute-start(f32[8,1,128]{2,0,1:T(8,128)S(1)} %get-tuple-element.25), channel_id=1, source_target_pairs={{0,16},{16,0},{32,48},{48,32},{64,80},{80,64},{96,112},{112,96},{1... | collective-permute-start | bytes 12296 | tf_op jit(solution)/shard_map/ppermute | solution.py:22
  94.6 10.9 %collective-permute-start.9 = (f32[8,1,128]{2,0,1:T(8,128)S(1)}, f32[8,1,128]{2,0,1:T(8,128)S(1)}, u32[]{:S(2)}, u32[]{:S(2)}) collective-permute-start(f32[8,1,128]{2,0,1:T(8,128)S(1)} %get-tuple-element.22), channel_id=1, source_target_pairs={{0,128},{128,0},{16,144},{144,16},{32,160},{160,32},{48,176},{176,... | collective-permute-start | bytes 12296 | tf_op jit(solution)/shard_map/ppermute | solution.py:22
  97.7 9.4 %collective-permute-start.8 = (f32[8,1,128]{2,0,1:T(8,128)S(1)}, f32[8,1,128]{2,0,1:T(8,128)S(1)}, u32[]{:S(2)}, u32[]{:S(2)}) collective-permute-start(f32[8,1,128]{2,0,1:T(8,128)S(1)} %get-tuple-element.23), channel_id=1, source_target_pairs={{0,64},{64,0},{16,80},{80,16},{32,96},{96,32},{48,112},{112,48},{1... | collective-permute-start | bytes 12296 | tf_op jit(solution)/shard_map/ppermute | solution.py:22
  99.6 8.2 %collective-permute-start.11 = (f32[8,1,128]{2,0,1:T(8,128)S(1)}, f32[8,1,128]{2,0,1:T(8,128)S(1)}, u32[]{:S(2)}, u32[]{:S(2)}) collective-permute-start(f32[8,1,128]{2,0,1:T(8,128)S(1)} %get-tuple-element.21), channel_id=1, source_target_pairs={{1,0},{2,1},{3,2},{4,3},{5,4},{6,5},{7,6},{8,7},{9,8},{10,9},{11,1... | collective-permute-start | bytes 12296 | tf_op jit(solution)/shard_map/ppermute | solution.py:35
  100.9 6.9 %collective-permute-start.10 = (f32[8,1,128]{2,0,1:T(8,128)S(1)}, f32[8,1,128]{2,0,1:T(8,128)S(1)}, u32[]{:S(2)}, u32[]{:S(2)}) collective-permute-start(f32[8,1,128]{2,0,1:T(8,128)S(1)} %get-tuple-element.21), channel_id=1, source_target_pairs={{0,1},{1,2},{2,3},{3,4},{4,5},{5,6},{6,7},{7,8},{8,9},{9,10},{10,1... | collective-permute-start | bytes 12296 | tf_op jit(solution)/shard_map/ppermute | solution.py:33
  142.7 15.3 %all-to-all-start.1 = ((f32[8,16,100]{2,0,1:T(8,128)}), f32[8,16,100]{2,0,1:T(8,128)S(1)}, u32[]{:S(2)}, u32[]{:S(2)}) async-start(f32[8,16,100]{2,0,1:T(8,128)} %copy.28), calls=%async_computation.1 | async-start | bytes 131072 | tf_op jit(solution)/shard_map/all_to_all | solution.py:76
where the time goes:
time: 160 us; the launch traced here: 159 us
  blocking collectives  86.5 us (54%)
  starting transfers between devices  47.6 us (30%)
  waiting for transfers between devices  11.1 us (7%)
  local copies, waits for them, and re-layouts  8.4 us (5%)
  other arithmetic  2.66 us (2%)
  matrix products  1.75 us (1%)
    all_gather x2, blocking collectives, shards(): lax.all_gather(right_side, 'period', axis=1, tiled=True)  70.6 us
    ppermute x8, starting transfers between devices, from_partner(): return lax.ppermute(block, axis, route)  29.7 us
    all_to_all x1, blocking collectives, shards(): lax.all_to_all(row_products, 'period', split_axis=1, concat_axis=2, tiled...  15.9 us
    ppermute x2, starting transfers between devices, padded_2(): lax.ppermute(tail, axis, [(i, (i + 1) % count) for i in range(ends)])  9.09 us
    all_to_all x1, waiting for transfers between devices, shards(): lax.all_to_all(row_products, 'period', split_axis=1, concat_axis=2, tiled...  8.41 us
    all_to_all x1, starting transfers between devices, shards(): lax.all_to_all(row_products, 'period', split_axis=1, concat_axis=2, tiled...  6.28 us
    gather x8, local copies, waits for them, and re-layouts, shards(): partner_block = jnp.take(received, partners[round_index], axis=0)  4.44 us
  transfers between devices with their start and end apart: 13, of which 3 were waited for; matrix products, arithmetic and copies ran while one was open for 4% of the time, Pallas kernels for 0%

commit v1 on v0

--- a/solution.py
+++ b/solution.py
@@ -10,6 +10,13 @@
 rho_ties = 1.0
 prox_weight = 0.5
 ramp_weight = 0.5
+
+
+def all_by_exchange(block, name, d):
+    count = lax.axis_size(name)
+    parts = jnp.stack([block for _ in range(count)])
+    parts = lax.all_to_all(parts, name, split_axis=0, concat_axis=0)
+    return jnp.concatenate(parts, axis=d)
 
 
 def from_partner(block, axis, apart):
@@ -69,7 +76,7 @@
         right_side = ((prox_weight * current - cost + addition) * live_mask).astype(jnp.bfloat16)
         row_products = jnp.einsum(
             "zpv,zrv->zpr",
-            lax.all_gather(right_side, "period", axis=1, tiled=True),
+            all_by_exchange(right_side, "period", 1),
             hinv,
             preferred_element_type=jnp.float32,
         )

time: 160 us -> 126 us (0.79)
  blocking collectives: 86.5 us -> 55 us
  starting transfers between devices: 47.6 us -> 44.7 us
    all_gather x2 -> x0, blocking collectives: 70.6 us -> none  [shards(): lax.all_gather(right_side, 'period', axis=1, tiled=True)]
    all_to_all x0 -> x2, blocking collectives: none -> 43.4 us  [all_by_exchange(): parts = lax.all_to_all(parts, name, split_axis=0, concat_axis=0)]
    all_to_all x1, blocking collectives: 15.9 us -> 11.7 us  [shards(): lax.all_to_all(row_products, 'period', split_axis=1, concat_axis=2, tiled...]
    all_to_all x1, starting transfers between devices: 6.28 us -> 3.5 us  [shards(): lax.all_to_all(row_products, 'period', split_axis=1, concat_axis=2, tiled...]
  transfers between devices with their start and end apart: 13 -> 13, of which waited for: 3 -> 3; matrix products, arithmetic and copies ran while one was open for 4% -> 5% of each run, Pallas kernels for 0% -> 0%
where the time goes in v1:
time: 126 us; the launch traced here: 125 us
  blocking collectives  55 us (44%)
  starting transfers between devices  44.7 us (35%)
  waiting for transfers between devices  11.3 us (9%)
  local copies, waits for them, and re-layouts  8.46 us (7%)
  other arithmetic  2.66 us (2%)
  matrix products  1.75 us (1%)
    all_to_all x2, blocking collectives, all_by_exchange(): parts = lax.all_to_all(parts, name, split_axis=0, concat_axis=0)  43.4 us
    ppermute x8, starting transfers between devices, from_partner(): return lax.ppermute(block, axis, route)  29.5 us
    all_to_all x1, blocking collectives, shards(): lax.all_to_all(row_products, 'period', split_axis=1, concat_axis=2, tiled...  11.7 us
    ppermute x2, starting transfers between devices, padded_2(): lax.ppermute(tail, axis, [(i, (i + 1) % count) for i in range(ends)])  9.09 us
    all_to_all x1, waiting for transfers between devices, shards(): lax.all_to_all(row_products, 'period', split_axis=1, concat_axis=2, tiled...  8.42 us
    gather x8, local copies, waits for them, and re-layouts, shards(): partner_block = jnp.take(received, partners[round_index], axis=0)  4.44 us
    all_to_all x1, starting transfers between devices, shards(): lax.all_to_all(row_products, 'period', split_axis=1, concat_axis=2, tiled...  3.5 us
    ppermute x8, waiting for transfers between devices, from_partner(): return lax.ppermute(block, axis, route)  2.81 us
  transfers between devices with their start and end apart: 13, of which 3 were waited for; matrix products, arithmetic and copies ran while one was open for 5% of the time, Pallas kernels for 0%

profile of v1, /device:TPU:6, one launch (start us, length us, event | category | flops | bytes accessed | tf_op | source)
XLA Modules:
  0.0 124.8 jit_solution(7314195584377905940)
XLA Ops:
  0.6 0.0 copy-start
  0.6 1.0 copy.24
  1.6 6.1 %collective-permute-start.1 = (f32[8,1,128]{2,0,1:T(8,128)S(1)}, f32[8,1,128]{2,0,1:T(8,128)S(1)}, u32[]{:S(2)}, u32[]{:S(2)}) collective-permute-start(f32[8,1,128]{2,0,1:T(8,128)S(1)} %get-tuple-element.32), channel_id=1, source_target_pairs={{0,32},{32,0},{16,48},{48,16},{64,96},{96,64},{80,112},{112,80},{1... | collective-permute-start | bytes 12296 | tf_op jit(solution)/shard_map/ppermute | solution.py:29
  7.7 1.9 %collective-permute-start = (f32[8,1,128]{2,0,1:T(8,128)S(1)}, f32[8,1,128]{2,0,1:T(8,128)S(1)}, u32[]{:S(2)}, u32[]{:S(2)}) collective-permute-start(f32[8,1,128]{2,0,1:T(8,128)S(1)} %get-tuple-element.33), channel_id=1, source_target_pairs={{0,16},{16,0},{32,48},{48,32},{64,80},{80,64},{96,112},{112,96},{1... | collective-permute-start | bytes 12296 | tf_op jit(solution)/shard_map/ppermute | solution.py:29
  9.6 0.8 compare_and_fusion
  10.5 0.7 fusion.15
  11.2 0.0 collective-permute-done.1
  11.2 0.6 gather_fusion.1
  11.8 0.0 collective-permute-done
  11.8 0.6 gather_fusion
  12.4 0.1 constant_dynamic-update-slice_fusion.5
  12.4 0.1 fusion.13
  12.5 2.7 %collective-permute-start.3 = (f32[8,1,128]{2,0,1:T(8,128)S(1)}, f32[8,1,128]{2,0,1:T(8,128)S(1)}, u32[]{:S(2)}, u32[]{:S(2)}) collective-permute-start(f32[8,1,128]{2,0,1:T(8,128)S(1)} %get-tuple-element.30), channel_id=1, source_target_pairs={{0,128},{128,0},{16,144},{144,16},{32,160},{160,32},{48,176},{176,... | collective-permute-start | bytes 12296 | tf_op jit(solution)/shard_map/ppermute | solution.py:29
  15.3 9.1 %collective-permute-start.2 = (f32[8,1,128]{2,0,1:T(8,128)S(1)}, f32[8,1,128]{2,0,1:T(8,128)S(1)}, u32[]{:S(2)}, u32[]{:S(2)}) collective-permute-start(f32[8,1,128]{2,0,1:T(8,128)S(1)} %get-tuple-element.31), channel_id=1, source_target_pairs={{0,64},{64,0},{16,80},{80,16},{32,96},{96,32},{48,112},{112,48},{1... | collective-permute-start | bytes 12296 | tf_op jit(solution)/shard_map/ppermute | solution.py:29
  24.4 1.3 %collective-permute-start.5 = (f32[8,1,128]{2,0,1:T(8,128)S(1)}, f32[8,1,128]{2,0,1:T(8,128)S(1)}, u32[]{:S(2)}, u32[]{:S(2)}) collective-permute-start(f32[8,1,128]{2,0,1:T(8,128)S(1)} %get-tuple-element.28), channel_id=1, source_target_pairs={{1,0},{2,1},{3,2},{4,3},{5,4},{6,5},{7,6},{8,7},{9,8},{10,9},{11,1... | collective-permute-start | bytes 12296 | tf_op jit(solution)/shard_map/ppermute | solution.py:42
  25.7 4.5 %collective-permute-start.4 = (f32[8,1,128]{2,0,1:T(8,128)S(1)}, f32[8,1,128]{2,0,1:T(8,128)S(1)}, u32[]{:S(2)}, u32[]{:S(2)}) collective-permute-start(f32[8,1,128]{2,0,1:T(8,128)S(1)} %get-tuple-element.28), channel_id=1, source_target_pairs={{0,1},{1,2},{2,3},{3,4},{4,5},{5,6},{6,7},{7,8},{8,9},{9,10},{10,1... | collective-permute-start | bytes 12296 | tf_op jit(solution)/shard_map/ppermute | solution.py:40
  30.3 0.0 collective-permute-done.3
  30.3 0.6 gather_fusion.3
  30.8 0.0 collective-permute-done.2
  30.8 0.6 gather_fusion.2
  31.4 0.1 constant_dynamic-update-slice_fusion.3
  31.5 0.1 constant_dynamic-update-slice_fusion.2
  31.5 0.0 collective-permute-done.5
  31.5 0.0 collective-permute-done.4
  31.6 0.0 copy-start.2
  31.6 0.9 fusion.10
  32.6 0.0 copy-start.1
  32.6 24.9 %all_to_all.34 = bf16[16,8,1,1600]{3,1,2,0:T(8,128)(2,1)S(1)} all-to-all(bf16[16,8,1,1600]{3,1,2,0:T(8,128)(2,1)S(1)} %stack.4), channel_id=1, replica_groups=mesh['zone'=32,'period'=16] {'period'}, dimensions={0} | all-to-all | bytes 819200 | tf_op jit(solution)/shard_map/all_to_all | solution.py:18
  57.4 0.0 copy-done
  57.4 0.9 fusion.2
  58.3 11.7 %all_to_all.35 = f32[8,16,100]{2,0,1:T(8,128)S(1)} all-to-all(f32[8,16,100]{2,0,1:T(8,128)S(1)} %copy.37), channel_id=1, replica_groups=mesh['zone'=32,'period'=16] {'period'}, dimensions={1} | all-to-all | bytes 102400 | tf_op jit(solution)/shard_map/all_to_all | solution.py:83
  70.0 0.1 all_to_all.26
  70.1 0.0 copy-done.2
  70.1 0.1 fusion.9
  70.2 2.4 %collective-permute-start.7 = (f32[8,1,128]{2,0,1:T(8,128)S(1)}, f32[8,1,128]{2,0,1:T(8,128)S(1)}, u32[]{:S(2)}, u32[]{:S(2)}) collective-permute-start(f32[8,1,128]{2,0,1:T(8,128)S(1)} %get-tuple-element.26), channel_id=1, source_target_pairs={{0,32},{32,0},{16,48},{48,16},{64,96},{96,64},{80,112},{112,80},{1... | collective-permute-start | bytes 12296 | tf_op jit(solution)/shard_map/ppermute | solution.py:29
  72.6 1.9 %collective-permute-start.6 = (f32[8,1,128]{2,0,1:T(8,128)S(1)}, f32[8,1,128]{2,0,1:T(8,128)S(1)}, u32[]{:S(2)}, u32[]{:S(2)}) collective-permute-start(f32[8,1,128]{2,0,1:T(8,128)S(1)} %get-tuple-element.27), channel_id=1, source_target_pairs={{0,16},{16,0},{32,48},{48,32},{64,80},{80,64},{96,112},{112,96},{1... | collective-permute-start | bytes 12296 | tf_op jit(solution)/shard_map/ppermute | solution.py:29
  74.6 2.0 %collective-permute-done.7 = f32[8,1,128]{2,0,1:T(8,128)S(1)} collective-permute-done((f32[8,1,128]{2,0,1:T(8,128)S(1)}, f32[8,1,128]{2,0,1:T(8,128)S(1)}, u32[]{:S(2)}, u32[]{:S(2)}) %collective-permute-start.7) | collective-permute-done | bytes 4128 | tf_op jit(solution)/shard_map/ppermute | solution.py:29
  76.6 0.6 gather_fusion.5
  77.1 0.0 collective-permute-done.6
  77.2 0.6 gather_fusion.4
  77.7 0.1 constant_dynamic-update-slice_fusion.11
  77.8 0.1 constant_dynamic-update-slice_fusion.10
  77.9 3.1 %collective-permute-start.9 = (f32[8,1,128]{2,0,1:T(8,128)S(1)}, f32[8,1,128]{2,0,1:T(8,128)S(1)}, u32[]{:S(2)}, u32[]{:S(2)}) collective-permute-start(f32[8,1,128]{2,0,1:T(8,128)S(1)} %get-tuple-element.24), channel_id=1, source_target_pairs={{0,128},{128,0},{16,144},{144,16},{32,160},{160,32},{48,176},{176,... | collective-permute-start | bytes 12296 | tf_op jit(solution)/shard_map/ppermute | solution.py:29
  81.0 2.2 %collective-permute-start.8 = (f32[8,1,128]{2,0,1:T(8,128)S(1)}, f32[8,1,128]{2,0,1:T(8,128)S(1)}, u32[]{:S(2)}, u32[]{:S(2)}) collective-permute-start(f32[8,1,128]{2,0,1:T(8,128)S(1)} %get-tuple-element.25), channel_id=1, source_target_pairs={{0,64},{64,0},{16,80},{80,16},{32,96},{96,32},{48,112},{112,48},{1... | collective-permute-start | bytes 12296 | tf_op jit(solution)/shard_map/ppermute | solution.py:29
  83.2 1.3 %collective-permute-start.11 = (f32[8,1,128]{2,0,1:T(8,128)S(1)}, f32[8,1,128]{2,0,1:T(8,128)S(1)}, u32[]{:S(2)}, u32[]{:S(2)}) collective-permute-start(f32[8,1,128]{2,0,1:T(8,128)S(1)} %get-tuple-element.23), channel_id=1, source_target_pairs={{1,0},{2,1},{3,2},{4,3},{5,4},{6,5},{7,6},{8,7},{9,8},{10,9},{11,1... | collective-permute-start | bytes 12296 | tf_op jit(solution)/shard_map/ppermute | solution.py:42
  84.5 4.5 %collective-permute-start.10 = (f32[8,1,128]{2,0,1:T(8,128)S(1)}, f32[8,1,128]{2,0,1:T(8,128)S(1)}, u32[]{:S(2)}, u32[]{:S(2)}) collective-permute-start(f32[8,1,128]{2,0,1:T(8,128)S(1)} %get-tuple-element.23), channel_id=1, source_target_pairs={{0,1},{1,2},{2,3},{3,4},{4,5},{5,6},{6,7},{7,8},{8,9},{9,10},{10,1... | collective-permute-start | bytes 12296 | tf_op jit(solution)/shard_map/ppermute | solution.py:40
  89.0 0.0 collective-permute-done.9
  89.0 0.6 gather_fusion.7
  89.6 0.8 collective-permute-done.8
  90.4 0.6 gather_fusion.6
  90.9 0.1 constant_dynamic-update-slice_fusion.9
  91.0 0.1 constant_dynamic-update-slice_fusion.8
  91.1 0.0 collective-permute-done.11
  91.1 0.0 collective-permute-done.10
  91.1 0.1 fusion.11
  91.3 18.5 %all_to_all.36 = bf16[16,8,1,1600]{3,1,2,0:T(8,128)(2,1)S(1)} all-to-all(bf16[16,8,1,1600]{3,1,2,0:T(8,128)(2,1)S(1)} %stack.5), channel_id=1, replica_groups=mesh['zone'=32,'period'=16] {'period'}, dimensions={0} | all-to-all | bytes 819200 | tf_op jit(solution)/shard_map/all_to_all | solution.py:18
  109.8 0.9 fusion
  110.7 0.7 copy.42
  111.3 3.5 %all-to-all-start.3 = ((f32[8,16,100]{2,0,1:T(8,128)}), f32[8,16,100]{2,0,1:T(8,128)S(1)}, u32[]{:S(2)}, u32[]{:S(2)}) async-start(f32[8,16,100]{2,0,1:T(8,128)} %copy.42), calls=%async_computation.3 | async-start | bytes 131072 | tf_op jit(solution)/shard_map/all_to_all | solution.py:83
  114.8 0.6 copy.45
  115.5 8.4 %all-to-all-done.3 = f32[8,16,100]{2,0,1:T(8,128)S(1)} async-done(((f32[8,16,100]{2,0,1:T(8,128)}), f32[8,16,100]{2,0,1:T(8,128)S(1)}, u32[]{:S(2)}, u32[]{:S(2)}) %all-to-all-start.3) | async-done | bytes 51232 | tf_op jit(solution)/shard_map/all_to_all | solution.py:83
  123.9 0.1 all_to_all.29
  124.0 0.1 fusion.8
  124.1 0.7 copy.44
  (16 shorter events, 0.2 us)
Async XLA Ops:
  0.6 56.8 %copy-start = (bf16[8,100,1600]{2,0,1:T(8,128)(2,1)S(1)}, bf16[8,100,1600]{2,0,1:T(8,128)(2,1)}, u32[]{:S(2)}) copy-start(bf16[8,100,1600]{2,0,1:T(8,128)(2,1)} %param.11) | copy-start | bytes 7680004
  1.6 9.6 %collective-permute-start.1 = (f32[8,1,128]{2,0,1:T(8,128)S(1)}, f32[8,1,128]{2,0,1:T(8,128)S(1)}, u32[]{:S(2)}, u32[]{:S(2)}) collective-permute-start(f32[8,1,128]{2,0,1:T(8,128)S(1)} %get-tuple-element.32), channel_id=1, source_target_pairs={{0,32},{32,0},{16,48},{48,16},{64,96},{96,64},{80,112},{112,80},{1... | collective-permute-start | bytes 12296 | tf_op jit(solution)/shard_map/ppermute | solution.py:29
  7.7 4.1 %collective-permute-start = (f32[8,1,128]{2,0,1:T(8,128)S(1)}, f32[8,1,128]{2,0,1:T(8,128)S(1)}, u32[]{:S(2)}, u32[]{:S(2)}) collective-permute-start(f32[8,1,128]{2,0,1:T(8,128)S(1)} %get-tuple-element.33), channel_id=1, source_target_pairs={{0,16},{16,0},{32,48},{48,32},{64,80},{80,64},{96,112},{112,96},{1... | collective-permute-start | bytes 12296 | tf_op jit(solution)/shard_map/ppermute | solution.py:29
  12.5 17.7 %collective-permute-start.3 = (f32[8,1,128]{2,0,1:T(8,128)S(1)}, f32[8,1,128]{2,0,1:T(8,128)S(1)}, u32[]{:S(2)}, u32[]{:S(2)}) collective-permute-start(f32[8,1,128]{2,0,1:T(8,128)S(1)} %get-tuple-element.30), channel_id=1, source_target_pairs={{0,128},{128,0},{16,144},{144,16},{32,160},{160,32},{48,176},{176,... | collective-permute-start | bytes 12296 | tf_op jit(solution)/shard_map/ppermute | solution.py:29
  15.3 15.6 %collective-permute-start.2 = (f32[8,1,128]{2,0,1:T(8,128)S(1)}, f32[8,1,128]{2,0,1:T(8,128)S(1)}, u32[]{:S(2)}, u32[]{:S(2)}) collective-permute-start(f32[8,1,128]{2,0,1:T(8,128)S(1)} %get-tuple-element.31), channel_id=1, source_target_pairs={{0,64},{64,0},{16,80},{80,16},{32,96},{96,32},{48,112},{112,48},{1... | collective-permute-start | bytes 12296 | tf_op jit(solution)/shard_map/ppermute | solution.py:29
  24.4 7.1 %collective-permute-start.5 = (f32[8,1,128]{2,0,1:T(8,128)S(1)}, f32[8,1,128]{2,0,1:T(8,128)S(1)}, u32[]{:S(2)}, u32[]{:S(2)}) collective-permute-start(f32[8,1,128]{2,0,1:T(8,128)S(1)} %get-tuple-element.28), channel_id=1, source_target_pairs={{1,0},{2,1},{3,2},{4,3},{5,4},{6,5},{7,6},{8,7},{9,8},{10,9},{11,1... | collective-permute-start | bytes 12296 | tf_op jit(solution)/shard_map/ppermute | solution.py:42
  25.7 5.9 %collective-permute-start.4 = (f32[8,1,128]{2,0,1:T(8,128)S(1)}, f32[8,1,128]{2,0,1:T(8,128)S(1)}, u32[]{:S(2)}, u32[]{:S(2)}) collective-permute-start(f32[8,1,128]{2,0,1:T(8,128)S(1)} %get-tuple-element.28), channel_id=1, source_target_pairs={{0,1},{1,2},{2,3},{3,4},{4,5},{5,6},{6,7},{7,8},{8,9},{9,10},{10,1... | collective-permute-start | bytes 12296 | tf_op jit(solution)/shard_map/ppermute | solution.py:40
  31.6 38.5 %copy-start.2 = (s32[8]{0:T(128)S(1)}, s32[8]{0:T(128)}, u32[]{:S(2)}) copy-start(s32[8]{0:T(128)} %param.12) | copy-start | bytes 100
  32.6 58.6 %copy-start.1 = (f32[8,1,1600]{2,1,0:T(1,128)S(1)}, f32[8,1,1600]{2,1,0:T(1,128)}, u32[]{:S(2)}) copy-start(f32[8,1,1600]{2,1,0:T(1,128)} %param.10) | copy-start | bytes 153604
  70.2 6.4 %collective-permute-start.7 = (f32[8,1,128]{2,0,1:T(8,128)S(1)}, f32[8,1,128]{2,0,1:T(8,128)S(1)}, u32[]{:S(2)}, u32[]{:S(2)}) collective-permute-start(f32[8,1,128]{2,0,1:T(8,128)S(1)} %get-tuple-element.26), channel_id=1, source_target_pairs={{0,32},{32,0},{16,48},{48,16},{64,96},{96,64},{80,112},{112,80},{1... | collective-permute-start | bytes 12296 | tf_op jit(solution)/shard_map/ppermute | solution.py:29
  72.6 4.5 %collective-permute-start.6 = (f32[8,1,128]{2,0,1:T(8,128)S(1)}, f32[8,1,128]{2,0,1:T(8,128)S(1)}, u32[]{:S(2)}, u32[]{:S(2)}) collective-permute-start(f32[8,1,128]{2,0,1:T(8,128)S(1)} %get-tuple-element.27), channel_id=1, source_target_pairs={{0,16},{16,0},{32,48},{48,32},{64,80},{80,64},{96,112},{112,96},{1... | collective-permute-start | bytes 12296 | tf_op jit(solution)/shard_map/ppermute | solution.py:29
  77.9 11.2 %collective-permute-start.9 = (f32[8,1,128]{2,0,1:T(8,128)S(1)}, f32[8,1,128]{2,0,1:T(8,128)S(1)}, u32[]{:S(2)}, u32[]{:S(2)}) collective-permute-start(f32[8,1,128]{2,0,1:T(8,128)S(1)} %get-tuple-element.24), channel_id=1, source_target_pairs={{0,128},{128,0},{16,144},{144,16},{32,160},{160,32},{48,176},{176,... | collective-permute-start | bytes 12296 | tf_op jit(solution)/shard_map/ppermute | solution.py:29
  81.0 9.4 %collective-permute-start.8 = (f32[8,1,128]{2,0,1:T(8,128)S(1)}, f32[8,1,128]{2,0,1:T(8,128)S(1)}, u32[]{:S(2)}, u32[]{:S(2)}) collective-permute-start(f32[8,1,128]{2,0,1:T(8,128)S(1)} %get-tuple-element.25), channel_id=1, source_target_pairs={{0,64},{64,0},{16,80},{80,16},{32,96},{96,32},{48,112},{112,48},{1... | collective-permute-start | bytes 12296 | tf_op jit(solution)/shard_map/ppermute | solution.py:29
  83.2 7.9 %collective-permute-start.11 = (f32[8,1,128]{2,0,1:T(8,128)S(1)}, f32[8,1,128]{2,0,1:T(8,128)S(1)}, u32[]{:S(2)}, u32[]{:S(2)}) collective-permute-start(f32[8,1,128]{2,0,1:T(8,128)S(1)} %get-tuple-element.23), channel_id=1, source_target_pairs={{1,0},{2,1},{3,2},{4,3},{5,4},{6,5},{7,6},{8,7},{9,8},{10,9},{11,1... | collective-permute-start | bytes 12296 | tf_op jit(solution)/shard_map/ppermute | solution.py:42
  84.5 6.6 %collective-permute-start.10 = (f32[8,1,128]{2,0,1:T(8,128)S(1)}, f32[8,1,128]{2,0,1:T(8,128)S(1)}, u32[]{:S(2)}, u32[]{:S(2)}) collective-permute-start(f32[8,1,128]{2,0,1:T(8,128)S(1)} %get-tuple-element.23), channel_id=1, source_target_pairs={{0,1},{1,2},{2,3},{3,4},{4,5},{5,6},{6,7},{7,8},{8,9},{9,10},{10,1... | collective-permute-start | bytes 12296 | tf_op jit(solution)/shard_map/ppermute | solution.py:40
  111.3 12.6 %all-to-all-start.3 = ((f32[8,16,100]{2,0,1:T(8,128)}), f32[8,16,100]{2,0,1:T(8,128)S(1)}, u32[]{:S(2)}, u32[]{:S(2)}) async-start(f32[8,16,100]{2,0,1:T(8,128)} %copy.42), calls=%async_computation.3 | async-start | bytes 131072 | tf_op jit(solution)/shard_map/all_to_all | solution.py:83
